TPU v7x, 128 devices: a whole 4x4x4 slice. The times are simulated.
128 devices in a mesh: lat: 16 (over y, z_hi, core), chan: 8 (over z_lo, x).
Axes of the slice: x: 4, y: 4, z: 4 (z_hi: 2, z_lo: 2; z = z_hi * 2 + z_lo), core: 2. Of those that a mesh axis runs over, the one named last changes fastest.
Arguments:
- state: bfloat16 [64, 512, 1024], P('lat', None, 'chan'), may hold values from -15 to 15
- background: bfloat16 [64, 512, 1024], P('lat', None, 'chan'), may hold values from -15.5 to 15.5
- gain: float32 [1024], replicated, may hold values from 0.5 to 2
- w_query: bfloat16 [1024, 1024], P(None, 'chan'), may hold values from -0.2 to 0.2
- w_key: bfloat16 [1024, 1024], P(None, 'chan'), may hold values from -5 to 5
- w_value: bfloat16 [1024, 1024], P(None, 'chan'), may hold values from -0.1875 to 0.1875
- w_out: bfloat16 [1024, 1024], P('chan'), may hold values from -0.75 to 0.75
- decoder: bfloat16 [1024, 69], P('chan'), may hold values from -0.1875 to 0.1875
- interp: bfloat16 [16, 8, 16, 16, 128, 128], P('lat', 'chan'), may hold values from -0.5 to 0.5
- obs_values: bfloat16 [16, 8, 16, 16, 128], P('lat', 'chan'), may hold values from -6 to 6
- tile_index: int32 [16, 8, 16, 16], P('lat', 'chan'), may hold values from 0 to 1103
- block_count: int32 [16, 8, 16], P('lat', 'chan'), may hold values from 1 to 16, as said below
Outputs:
- misfit: float32 [16, 8, 16, 16, 128], P(None, 'chan', 'lat')
- gradient: float32 [64, 512, 1024], P('lat', None, 'chan')
Inputs may be any that keep to these rules, and one draw needn't show every extreme that they name: `tile_index`: A tile index n names variable n // 16 and the run n % 16 of 128 tokens of the target band. Live slots are the first block_count ones; every draw has a target band that receives 16 blocks from every owner and channel group.
All inputs are finite; a program needn't handle non-finite values.
Results may differ from a plain program's by a relative error of at most 0.02.
The roundings to bfloat16 on the way count: a program that leaves them out, or rounds other values in their place, can miss the bound.
Values may be sent and summed in bfloat16 or wider, within the bound.
A program may use at most 128 MiB of HBM per device.

v0:
```python
import jax
import jax.numpy as jnp
from jax import lax
from jax.sharding import PartitionSpec as P

D = 1024
HD = 64
VARS = 69
CELLS = 128
WC = 256
NC = 512
EPSILON = 1e-05
NEGATIVE = -1e30


def with_halo(array, sides, width):
    for axis, dim in sides:
        size, length = (lax.axis_size(axis), array.shape[dim])
        up = [(i, (i + 1) % size) for i in range(size - 1)]
        down = [(j, i) for i, j in up]
        last = lax.slice_in_dim(array, length - width, length, axis=dim)
        initial = lax.slice_in_dim(array, 0, width, axis=dim)
        before = lax.ppermute(last, axis, up)
        after = lax.ppermute(initial, axis, down)
        array = jnp.concatenate([before, array, after], axis=dim)
    return array


def in_blocks(array, dim, length):
    lengths = array.shape
    parts = array.reshape(*lengths[:dim], length, lengths[dim] // length, *lengths[dim + 1 :])
    return jnp.moveaxis(parts, dim, 0)


def sent_and_summed(array, axis, dim):
    length = lax.axis_size(axis)
    parts = lax.all_to_all(in_blocks(array, dim, length), axis, 0, 0, tiled=True)
    return jnp.sum(parts.astype(jnp.float32), axis=0)


def from_everyone(array, axis):
    copies = jnp.broadcast_to(array, (lax.axis_size(axis), *array.shape))
    return lax.all_to_all(copies, axis, split_axis=0, concat_axis=0, tiled=True)


def of_everyone(array, axis):
    everything = from_everyone(array, axis)
    return jnp.sum(everything.astype(jnp.float32), axis=0)


def in_one_piece(arrays, axis, split_dim, concat_dim, along):
    ends, at = ([], 0)
    for a in arrays[:-1]:
        at += a.shape[along]
        ends.append(at)
    both = jnp.concatenate(arrays, axis=along)
    return tuple(
        jnp.split(
            lax.all_to_all(both, axis, split_axis=split_dim, concat_axis=concat_dim, tiled=True),
            ends,
            axis=along,
        )
    )


def taken_together(array, axis):
    everything = from_everyone(array, axis)
    return jnp.sum(everything, axis=0)


def in_one(arrays, axis):
    ends = [0]
    for a in arrays:
        ends.append(ends[-1] + a.size)
    total = taken_together(jnp.concatenate([a.ravel() for a in arrays]), axis)
    return tuple((total[b:e].reshape(a.shape) for a, b, e in zip(arrays, ends, ends[1:])))


def normalize(state_rows):
    average = jnp.mean(state_rows, axis=-1, keepdims=True)
    centred = state_rows - average
    variance = jnp.mean(centred * centred, axis=-1, keepdims=True)
    inverse = lax.rsqrt(variance + EPSILON)
    return (centred * inverse, inverse)


def window_keys(padded, rows_band):
    stacked = jnp.stack(
        [padded[0:rows_band], padded[1 : rows_band + 1], padded[2 : rows_band + 2]], axis=1
    )
    shaped = stacked.reshape(rows_band, 3, NC // WC, WC, stacked.shape[3], stacked.shape[4])
    shaped = jnp.transpose(shaped, (0, 2, 1, 3, 4, 5))
    return shaped.reshape(rows_band, NC // WC, 3 * WC, stacked.shape[3], stacked.shape[4])


def key_mask(valid_rows):
    rows_band = valid_rows.shape[0] - 2
    triple = jnp.stack(
        [valid_rows[0:rows_band], valid_rows[1 : rows_band + 1], valid_rows[2 : rows_band + 2]],
        axis=1,
    )
    spread = jnp.repeat(triple, WC, axis=1)
    return spread[:, None, None, None, :]


def attend_forward(queries, keys_win, values_win, key_valid):
    scores = jnp.einsum(
        "rwihd,rwjhd->rwhij", queries, keys_win, preferred_element_type=jnp.float32
    ) * HD ** (-0.5)
    scores = jnp.where(key_valid, scores, NEGATIVE)
    highest = jnp.max(scores, axis=-1, keepdims=True)
    exponent = jnp.exp(scores - highest)
    attention = exponent / jnp.sum(exponent, axis=-1, keepdims=True)
    attention_low = attention.astype(jnp.bfloat16)
    mixed_heads = jnp.einsum(
        "rwhij,rwjhd->rwihd", attention_low, values_win, preferred_element_type=jnp.float32
    ).astype(jnp.bfloat16)
    return (attention, attention_low, mixed_heads)


def attend_backward(queries, keys_win, values_win, attention, attention_low, grad_mixed):
    grad_probs = jnp.einsum(
        "rwihd,rwjhd->rwhij", grad_mixed, values_win, preferred_element_type=jnp.float32
    )
    row_delta = jnp.sum(attention * grad_probs, axis=-1, keepdims=True)
    grad_scores = (attention * (grad_probs - row_delta) * HD ** (-0.5)).astype(jnp.bfloat16)
    grad_queries = jnp.einsum(
        "rwhij,rwjhd->rwihd", grad_scores, keys_win, preferred_element_type=jnp.float32
    ).astype(jnp.bfloat16)
    grad_keys = jnp.einsum(
        "rwhij,rwihd->rwjhd", grad_scores, queries, preferred_element_type=jnp.float32
    )
    grad_values = jnp.einsum(
        "rwhij,rwihd->rwjhd", attention_low, grad_mixed, preferred_element_type=jnp.float32
    )
    return (grad_queries, grad_keys, grad_values)


def unwindow(windowed, rows_band):
    width_heads = windowed.shape[3] * windowed.shape[4]
    shaped = windowed.reshape(rows_band, NC // WC, 3, WC, width_heads)
    shaped = jnp.transpose(shaped, (0, 2, 1, 3, 4)).reshape(rows_band, 3, NC, width_heads)
    summed = jnp.zeros((rows_band + 2, NC, width_heads), jnp.float32)
    for offset in range(3):
        summed = summed.at[offset : offset + rows_band].add(shaped[:, offset])
    return summed


def contract_last(left_rows, right_rows):
    return lax.dot_general(
        left_rows, right_rows, (((1,), (1,)), ((), ())), preferred_element_type=jnp.float32
    )


def body(
    state,
    background,
    gain,
    w_query,
    w_key,
    w_value,
    w_out,
    decoder,
    interp,
    obs_values,
    tile_index,
    block_count,
):
    rows_band, columns, width_local = state.shape
    tokens = rows_band * columns
    heads_local = width_local // HD
    chan_pos = lax.axis_index("chan")
    lat_pos = lax.axis_index("lat")
    lat_count = lax.axis_size("lat")
    wide_state = lax.all_gather(state, "chan", axis=2, tiled=True)
    hat_rows, inverse = normalize(wide_state.astype(jnp.float32).reshape(tokens, D))
    normed = (hat_rows * gain).astype(jnp.bfloat16)
    queries = jnp.dot(normed, w_query, preferred_element_type=jnp.float32).astype(jnp.bfloat16)
    keys_local = jnp.dot(normed, w_key, preferred_element_type=jnp.float32).astype(jnp.bfloat16)
    values_local = jnp.dot(normed, w_value, preferred_element_type=jnp.float32).astype(jnp.bfloat16)
    key_pair = jnp.stack([keys_local, values_local]).reshape(2, rows_band, columns, width_local)
    padded = with_halo(key_pair, (("lat", 1),), 1)
    global_rows = lat_pos * rows_band + jnp.arange(rows_band + 2, dtype=jnp.int32) - 1
    valid_rows = (global_rows >= 0) & (global_rows < lat_count * rows_band)
    key_valid = key_mask(valid_rows)
    keys_win = window_keys(padded[0].reshape(rows_band + 2, columns, heads_local, HD), rows_band)
    values_win = window_keys(padded[1].reshape(rows_band + 2, columns, heads_local, HD), rows_band)
    query_win = queries.reshape(rows_band, columns // WC, WC, heads_local, HD)
    attention, attention_low, mixed_heads = attend_forward(
        query_win, keys_win, values_win, key_valid
    )
    attn_part = jnp.dot(
        mixed_heads.reshape(tokens, width_local), w_out, preferred_element_type=jnp.float32
    )
    attn_sum = sent_and_summed(
        attn_part.reshape(rows_band, columns, D).astype(jnp.bfloat16), "chan", 2
    )
    updated = (state.astype(jnp.float32) + attn_sum).astype(jnp.bfloat16)
    fields_part = lax.dot_general(
        decoder,
        updated.reshape(tokens, width_local),
        (((0,), (1,)), ((), ())),
        preferred_element_type=jnp.float32,
    )
    fields = of_everyone(fields_part.astype(jnp.bfloat16), "chan").astype(jnp.float32)
    tiles_here = fields.astype(jnp.bfloat16).reshape(VARS * (tokens // CELLS), CELLS)
    slot_ids = jnp.arange(tile_index.shape[-1], dtype=jnp.int32)
    tiles_in = lax.all_to_all(tile_index, "lat", split_axis=2, concat_axis=0, tiled=True)
    sent_tiles = tiles_here[tiles_in]
    picked = lax.all_to_all(sent_tiles, "lat", split_axis=0, concat_axis=2, tiled=True)
    predicted = jnp.einsum(
        "abcsok,abcsk->abcso", interp, picked, preferred_element_type=jnp.float32
    )
    live_slot = slot_ids < block_count[..., None]
    own_misfit = jnp.where(live_slot[..., None], predicted - obs_values.astype(jnp.float32), 0.0)
    own_adjoint = jnp.einsum(
        "abcsok,abcso->abcsk",
        interp,
        own_misfit.astype(jnp.bfloat16),
        preferred_element_type=jnp.float32,
    )
    adjoint, misfit = tuple(
        (
            part.astype(jnp.float32)
            for part in in_one_piece(
                (own_adjoint.astype(jnp.bfloat16), own_misfit.astype(jnp.bfloat16)), "lat", 2, 0, 1
            )
        )
    )
    grad_tiles = (
        jnp.zeros((tiles_here.shape[0], CELLS), jnp.float32)
        .at[tiles_in.reshape(-1)]
        .add(adjoint.reshape(-1, CELLS))
    )
    grad_tiles = of_everyone(grad_tiles.astype(jnp.bfloat16), "chan").astype(jnp.float32)
    grad_field = grad_tiles.reshape(VARS, tokens)
    grad_update = lax.dot_general(
        grad_field,
        decoder.astype(jnp.float32),
        (((0,), (1,)), ((), ())),
        precision=lax.Precision.HIGHEST,
    )
    grad_low = grad_update.astype(jnp.bfloat16).reshape(rows_band, columns, width_local)
    portion = lax.all_gather(grad_low, "chan", axis=2, tiled=True)
    grad_mixed = contract_last(portion.reshape(tokens, portion.shape[2]), w_out)
    grad_mixed = grad_mixed.astype(jnp.bfloat16).reshape(
        rows_band, columns // WC, WC, heads_local, HD
    )
    grad_queries, grad_keys_win, grad_values_win = attend_backward(
        query_win, keys_win, values_win, attention, attention_low, grad_mixed
    )
    grad_pair = jnp.stack(
        [unwindow(grad_keys_win, rows_band), unwindow(grad_values_win, rows_band)]
    )
    rim_rows = jnp.stack([grad_pair[:, 0], grad_pair[:, rows_band + 1]], axis=1)
    arrived = with_halo(rim_rows.astype(jnp.bfloat16), (("lat", 1),), 1).astype(rim_rows.dtype)
    own_rows = grad_pair[:, 1 : rows_band + 1]
    own_rows = own_rows.at[:, 0].add(arrived[:, 0])
    own_rows = own_rows.at[:, rows_band - 1].add(arrived[:, 3])
    grad_keys = own_rows[0].astype(jnp.bfloat16).reshape(tokens, width_local)
    grad_values = own_rows[1].astype(jnp.bfloat16).reshape(tokens, width_local)
    grad_part = contract_last(grad_queries.reshape(tokens, width_local), w_query)
    grad_part = grad_part + contract_last(grad_keys, w_key)
    grad_part = grad_part + contract_last(grad_values, w_value)
    grad_normed = lax.psum_scatter(
        grad_part.astype(jnp.bfloat16), "chan", scatter_dimension=1, tiled=True
    ).astype(jnp.float32)
    gain_local = lax.dynamic_slice_in_dim(gain, chan_pos * width_local, width_local, 0)
    hat_local = lax.dynamic_slice_in_dim(hat_rows, chan_pos * width_local, width_local, 1)
    grad_hat = grad_normed * gain_local
    row_sum, cross_sum = in_one(
        (
            jnp.sum(grad_hat, axis=-1, keepdims=True),
            jnp.sum(grad_hat * hat_local, axis=-1, keepdims=True),
        ),
        "chan",
    )
    grad_norm = (grad_hat - row_sum / D - hat_local * (cross_sum / D)) * inverse
    state_flat = state.astype(jnp.float32).reshape(tokens, width_local)
    gradient = (
        state_flat
        - background.astype(jnp.float32).reshape(tokens, width_local)
        + grad_update
        + grad_norm
    )
    return (misfit, gradient.reshape(rows_band, columns, width_local))


def solution(mesh):
    return jax.shard_map(
        body,
        mesh=mesh,
        in_specs=(
            P("lat", None, "chan"),
            P("lat", None, "chan"),
            P(),
            P(None, "chan"),
            P(None, "chan"),
            P(None, "chan"),
            P("chan", None),
            P("chan", None),
            P("lat", "chan", None, None, None, None),
            P("lat", "chan", None, None, None),
            P("lat", "chan", None, None),
            P("lat", "chan", None),
        ),
        out_specs=(P(None, "chan", "lat", None, None), P("lat", None, "chan")),
        check_vma=False,
    )
```

profile of v0, /device:TPU:0, one launch (start us, length us, event | category | flops | bytes accessed | tf_op | source)
XLA Modules:
  0.0 622.9 jit_solution(2726166261618390722)
XLA Ops:
  8.0 63.6 %all-gather.3.cloned.1.call-done = bf16[4,512,1024]{2,1,0:T(8,128)(2,1)} async-done(((bf16[4,512,128]{2,1,0:T(8,128)(2,1)}), bf16[4,512,1024]{2,1,0:T(8,128)(2,1)}) %all-gather.3.cloned.1.call-update) | async-done | bytes 4194320 | tf_op jit(solution)/shard_map/all_gather | solution.py:175
  94.3 4.3 convolution_convert_fusion.1
  127.8 10.2 %fusion.81 = (f32[4,2,2,256]{3,2,1,0:T(2,128)S(1)}, f32[4,2,2,256,768]{4,3,2,1,0:T(8,128)}) fusion(pred[4,768]{1,0:T(4,128)(4,1)S(1)} %bitcast.246, bf16[4,2,256,2,64]{2,4,3,1,0:T(8,128)(2,1)S(1)} %copy-done.15, bf16[4,2,768,2,64]{2,4,3,1,0:T(8,128)(2,1)} %reshape.530), kind=kOutput, calls=%fused_computation.131 | convolution fusion | flops 415236864 | bytes 14699520 | tf_op jit(solution)/shard_map/sub | solution.py:112
  138.0 6.7 %fusion.41 = bf16[4,2,256,2,64]{2,4,3,1,0:T(8,128)(2,1)S(1)} fusion(bf16[4,2,768,2,64]{2,4,3,1,0:T(8,128)(2,1)S(1)} %copy-done.4, f32[4,2,2,256,768]{4,3,2,1,0:T(8,128)} %get-tuple-element.134, f32[4,2,2,256]{3,2,1,0:T(2,128)S(1)} %get-tuple-element.133), kind=kOutput, calls=%fused_computation.56 | convolution fusion | flops 409206784 | bytes 14696448 | tf_op jit(solution)/shard_map/rwhij,rwjhd->rwihd/dot_general | solution.py:115
  148.0 54.5 %all_to_all.60 = bf16[8,4,512,128]{3,2,1,0:T(8,128)(2,1)} all-to-all(bf16[8,4,512,128]{3,2,1,0:T(8,128)(2,1)S(1)} %bitcast.221), channel_id=1, replica_groups=mesh['lat'=16,'chan'=8] {'chan'}, dimensions={0} | all-to-all | bytes 8388608 | tf_op jit(solution)/shard_map/all_to_all | solution.py:37
  202.5 9.4 %all-to-all-start.2 = ((s32[1,1,16,16]{3,1,0,2:T(1,128)}), s32[1,1,16,16]{3,1,0,2:T(1,128)S(1)}, u32[]{:S(2)}, u32[]{:S(2)}) async-start(s32[1,1,16,16]{3,1,0,2:T(1,128)} %bitcast.15), calls=%async_computation.2 | async-start | bytes 16384 | tf_op jit(solution)/shard_map/all_to_all | solution.py:208
  224.9 29.9 %all-to-all-done.1 = bf16[8,69,2048]{2,1,0:T(8,128)(2,1)S(1)} async-done(((bf16[8,69,2048]{2,1,0:T(8,128)(2,1)}), bf16[8,69,2048]{2,1,0:T(8,128)(2,1)S(1)}, u32[]{:S(2)}, u32[]{:S(2)}) %all-to-all-start.1) | async-done | bytes 2261024 | tf_op jit(solution)/shard_map/all_to_all | solution.py:43
  256.9 4.9 all-to-all-start.3
  263.1 6.4 %all-to-all-done.3 = bf16[16,1,1,16,128]{4,3,2,1,0:T(8,128)(2,1)S(1)} async-done(((bf16[16,1,1,16,128]{4,3,2,1,0:T(8,128)(2,1)}), bf16[16,1,1,16,128]{4,3,2,1,0:T(8,128)(2,1)S(1)}, u32[]{:S(2)}, u32[]{:S(2)}) %all-to-all-start.3) | async-done | bytes 65568 | tf_op jit(solution)/shard_map/all_to_all | solution.py:210
  269.5 7.8 %fusion.6 = f32[16,16,1,128]{3,2,1,0:T(1,128)S(1)} fusion(bf16[1,1,16,16,128,128]{5,4,3,2,1,0:T(8,128)(2,1)} %param.36, bf16[16,16,128,1]{2,1,0,3:T(8,128)(2,1)S(1)} %bitcast.237), kind=kOutput, calls=%fused_computation.12 | convolution fusion | flops 8388608 | bytes 8585216 | tf_op jit(solution)/shard_map/abcsok,abcsk->abcso/dot_general | solution.py:211
  277.4 5.7 fusion.4
  287.3 7.9 %all-to-all-done.4 = bf16[1,2,16,16,128]{4,3,1,0,2:T(8,128)(2,1)S(1)} async-done(((bf16[1,2,16,16,128]{4,3,1,0,2:T(8,128)(2,1)}), bf16[1,2,16,16,128]{4,3,1,0,2:T(8,128)(2,1)S(1)}, u32[]{:S(2)}, u32[]{:S(2)}) %all-to-all-start.4) | async-done | bytes 131104 | tf_op jit(solution)/shard_map/all_to_all | solution.py:59
  297.8 37.8 %all_to_all.61 = bf16[8,1104,128]{2,1,0:T(8,128)(2,1)S(1)} all-to-all(bf16[8,1104,128]{2,1,0:T(8,128)(2,1)S(1)} %broadcast_in_dim.61), channel_id=1, replica_groups=mesh['lat'=16,'chan'=8] {'chan'}, dimensions={0} | all-to-all | bytes 4521984 | tf_op jit(solution)/shard_map/all_to_all | solution.py:43
  338.3 55.6 %all-gather.5.cloned.1.call-done = bf16[4,512,1024]{2,1,0:T(8,128)(2,1)} async-done(((bf16[4,512,128]{2,1,0:T(8,128)(2,1)}), bf16[4,512,1024]{2,1,0:T(8,128)(2,1)}) %all-gather.5.cloned.1.call-update) | async-done | bytes 4194320 | tf_op jit(solution)/shard_map/all_gather | solution.py:244
  399.7 6.5 %fusion.30 = f32[4,2,768,2,64]{2,4,3,1,0:T(8,128)S(1)} fusion(bf16[4,2,256,2,64]{2,4,3,1,0:T(8,128)(2,1)} %copy.154, f32[4,2,2,256,768]{4,3,2,1,0:T(8,128)} %get-tuple-element.134, f32[4,2,2,256]{3,2,1,0:T(2,128)S(1)} %get-tuple-element.133), kind=kOutput, calls=%fused_computation.48 | convolution fusion | flops 408944640 | bytes 16269312 | tf_op jit(solution)/shard_map/rwhij,rwihd->rwjhd/dot_general | solution.py:133
  406.3 6.3 %fusion.83 = f32[4,2,2,256,768]{4,3,2,1,0:T(8,128)} fusion(bf16[4,2,256,2,64]{2,4,3,1,0:T(8,128)(2,1)S(1)} %copy-done.10, bf16[4,2,768,2,64]{2,4,3,1,0:T(8,128)(2,1)S(1)} %copy-done.5), kind=kOutput, calls=%fused_computation.133 | convolution fusion | flops 402653184 | bytes 14680064 | tf_op jit(solution)/shard_map/rwihd,rwjhd->rwhij/dot_general | solution.py:122
  412.6 33.2 %fusion.44 = bf16[4,2,256,2,64]{2,4,3,1,0:T(8,128)(2,1)} fusion(bf16[4,2,768,2,64]{2,4,3,1,0:T(8,128)(2,1)} %reshape.530, f32[4,2,2,256,768]{4,3,2,1,0:T(8,128)} %fusion.83, f32[4,2,2,256,768]{4,3,2,1,0:T(8,128)} %get-tuple-element.134, f32[4,2,2,256]{3,2,1,0:T(2,128)S(1)} %get-tuple-element.133), kind=kOutput, calls=%fused_computation.57 | convolution fusion | flops 424940288 | bytes 27279360 | tf_op jit(solution)/shard_map/rwhij,rwjhd->rwihd/dot_general | solution.py:127
  445.8 40.1 %fusion.27 = f32[4,2,768,2,64]{2,4,3,1,0:T(8,128)} fusion(bf16[4,2,256,2,64]{2,4,3,1,0:T(8,128)(2,1)} %copy.145, f32[4,2,2,256,768]{4,3,2,1,0:T(8,128)} %fusion.83, f32[4,2,2,256,768]{4,3,2,1,0:T(8,128)} %get-tuple-element.134, f32[4,2,2,256]{3,2,1,0:T(2,128)S(1)} %get-tuple-element.133), kind=kOutput, calls=%fused_computation.47 | convolution fusion | flops 424678144 | bytes 28852224 | tf_op jit(solution)/shard_map/rwhij,rwihd->rwjhd/dot_general | solution.py:130
  485.9 5.9 reshape.545
  491.8 4.9 copy.177
  496.7 4.9 copy.157
  534.2 6.5 %copy.182 = bf16[2048,1024]{0,1:T(8,128)(2,1)} copy(bf16[2048,1024]{1,0:T(8,128)(2,1)} %add_convert_fusion) | data formatting | bytes 8388608
  541.7 59.0 %reduce-scatter.4.cloned.1.call-done = bf16[128,2048]{1,0:T(8,128)(2,1)} async-done(((bf16[1024,2048]{1,0:T(8,128)(2,1)}), bf16[128,2048]{1,0:T(8,128)(2,1)}) %reduce-scatter.4.cloned.1.call-update) | async-done | bytes 524304
  604.0 9.1 %all_to_all.62 = f32[8,1,4096]{2,1,0:T(1,128)S(1)} all-to-all(f32[8,1,4096]{2,1,0:T(1,128)S(1)} %broadcast_in_dim.62), channel_id=1, replica_groups=mesh['lat'=16,'chan'=8] {'chan'}, dimensions={0} | all-to-all | bytes 262144 | tf_op jit(solution)/shard_map/all_to_all | solution.py:43
  (169 shorter events, 127.0 us)
Async XLA Ops:
  7.2 138.4 %copy-start = (bf16[128,1024]{1,0:T(8,128)(2,1)S(1)}, bf16[128,1024]{1,0:T(8,128)(2,1)}, u32[]{:S(2)}) copy-start(bf16[128,1024]{1,0:T(8,128)(2,1)} %param.34) | copy-start | bytes 786436
  7.2 64.5 %all-gather.3.cloned.1.call-start = ((), (), s32[]{:S(2)}) async-start(), calls=%async_computation.8 | async-start | bytes 4718592 | tf_op jit(solution)/shard_map/all_gather | solution.py:175
  8.0 68.5 %copy-start.26 = (f32[1024]{0:T(1024)S(1)}, f32[1024]{0:T(1024)}, u32[]{:S(2)}) copy-start(f32[1024]{0:T(1024)} %param.30) | copy-start | bytes 12292
  90.8 18.1 %collective-permute-start = (bf16[2,1,512,128]{2,3,1,0:T(8,128)(2,1)}, bf16[2,1,512,128]{2,3,1,0:T(8,128)(2,1)}, u32[]{:S(2)}, u32[]{:S(2)}) collective-permute-start(bf16[2,1,512,128]{2,3,1,0:T(8,128)(2,1)} %get-tuple-element.120), channel_id=1, source_target_pairs={{0,8},{8,16},{16,24},{24,32},{32,40},{40,48},{48,56},{56,64},{64,7... | collective-permute-start | bytes 786440 | tf_op jit(solution)/shard_map/ppermute | solution.py:23
  92.8 16.1 %collective-permute-start.1 = (bf16[2,1,512,128]{2,3,1,0:T(8,128)(2,1)}, bf16[2,1,512,128]{2,3,1,0:T(8,128)(2,1)}, u32[]{:S(2)}, u32[]{:S(2)}) collective-permute-start(bf16[2,1,512,128]{2,3,1,0:T(8,128)(2,1)} %get-tuple-element.121), channel_id=1, source_target_pairs={{8,0},{16,8},{24,16},{32,24},{40,32},{48,40},{56,48},{64,56},{72,6... | collective-permute-start | bytes 786440 | tf_op jit(solution)/shard_map/ppermute | solution.py:24
  127.8 10.2 %copy-start.4 = (bf16[4,2,768,2,64]{2,4,3,1,0:T(8,128)(2,1)S(1)}, bf16[4,2,768,2,64]{2,4,3,1,0:T(8,128)(2,1)}, u32[]{:S(2)}) copy-start(bf16[4,2,768,2,64]{2,4,3,1,0:T(8,128)(2,1)} %reshape.528) | copy-start | bytes 4718596
  202.5 12.3 %copy-start.11 = (bf16[4,512,128]{2,1,0:T(8,128)(2,1)S(1)}, bf16[4,512,128]{2,1,0:T(8,128)(2,1)}, u32[]{:S(2)}) copy-start(bf16[4,512,128]{2,1,0:T(8,128)(2,1)} %param.28) | copy-start | bytes 1572868
  202.5 12.3 %copy-start.14 = (bf16[4,512,128]{2,1,0:T(8,128)(2,1)S(1)}, bf16[4,512,128]{2,1,0:T(8,128)(2,1)}, u32[]{:S(2)}) copy-start(bf16[4,512,128]{2,1,0:T(8,128)(2,1)} %param.29) | copy-start | bytes 1572868
  202.5 16.9 %all-to-all-start.2 = ((s32[1,1,16,16]{3,1,0,2:T(1,128)}), s32[1,1,16,16]{3,1,0,2:T(1,128)S(1)}, u32[]{:S(2)}, u32[]{:S(2)}) async-start(s32[1,1,16,16]{3,1,0,2:T(1,128)} %bitcast.15), calls=%async_computation.2 | async-start | bytes 16384 | tf_op jit(solution)/shard_map/all_to_all | solution.py:208
  221.1 40.7 %copy-start.27 = (s32[1,1,16]{2,1,0:T(1,128)S(1)}, s32[1,1,16]{2,1,0:T(1,128)}, u32[]{:S(2)}) copy-start(s32[1,1,16]{2,1,0:T(1,128)} %param.39) | copy-start | bytes 196
  221.1 33.7 %all-to-all-start.1 = ((bf16[8,69,2048]{2,1,0:T(8,128)(2,1)}), bf16[8,69,2048]{2,1,0:T(8,128)(2,1)S(1)}, u32[]{:S(2)}, u32[]{:S(2)}) async-start(bf16[8,69,2048]{2,1,0:T(8,128)(2,1)} %broadcast_in_dim.58), calls=%async_computation.1 | async-start | bytes 4718592 | tf_op jit(solution)/shard_map/all_to_all | solution.py:43
  256.9 12.6 %all-to-all-start.3 = ((bf16[16,1,1,16,128]{4,3,2,1,0:T(8,128)(2,1)}), bf16[16,1,1,16,128]{4,3,2,1,0:T(8,128)(2,1)S(1)}, u32[]{:S(2)}, u32[]{:S(2)}) async-start(bf16[16,1,1,16,128]{4,3,2,1,0:T(8,128)(2,1)} %bitcast.18), calls=%async_computation.3 | async-start | bytes 131072 | tf_op jit(solution)/shard_map/all_to_all | solution.py:210
  269.5 7.8 %copy-start.25 = (bf16[1,1,16,16,128]{4,3,2,1,0:T(8,128)(2,1)S(1)}, bf16[1,1,16,16,128]{4,3,2,1,0:T(8,128)(2,1)}, u32[]{:S(2)}) copy-start(bf16[1,1,16,16,128]{4,3,2,1,0:T(8,128)(2,1)} %param.37) | copy-start | bytes 196612
  283.8 11.5 %all-to-all-start.4 = ((bf16[1,2,16,16,128]{4,3,1,0,2:T(8,128)(2,1)}), bf16[1,2,16,16,128]{4,3,1,0,2:T(8,128)(2,1)S(1)}, u32[]{:S(2)}, u32[]{:S(2)}) async-start(bf16[1,2,16,16,128]{4,3,1,0,2:T(8,128)(2,1)} %pad_maximum_fusion.12), calls=%async_computation.4 | async-start | bytes 262144 | tf_op jit(solution)/shard_map/all_to_all | solution.py:59
  287.3 106.6 %all-gather.5.cloned.1.call-start = ((), (), s32[]{:S(2)}) async-start(), calls=%async_computation.9 | async-start | bytes 4718592 | tf_op jit(solution)/shard_map/all_gather | solution.py:244
  338.3 262.4 %reduce-scatter.4.cloned.1.call-start = ((), (), s32[]{:S(2)}) async-start(), calls=%async_computation.10 | async-start | bytes 4718592
  399.7 6.5 %copy-start.5 = (bf16[4,2,768,2,64]{2,4,3,1,0:T(8,128)(2,1)S(1)}, bf16[4,2,768,2,64]{2,4,3,1,0:T(8,128)(2,1)}, u32[]{:S(2)}) copy-start(bf16[4,2,768,2,64]{2,4,3,1,0:T(8,128)(2,1)} %reshape.528) | copy-start | bytes 4718596
  399.7 6.6 %copy-start.10 = (bf16[4,2,256,2,64]{2,4,3,1,0:T(8,128)(2,1)S(1)}, bf16[4,2,256,2,64]{2,4,3,1,0:T(8,128)(2,1)}, u32[]{:S(2)}) copy-start(bf16[4,2,256,2,64]{2,4,3,1,0:T(8,128)(2,1)} %copy.154) | copy-start | bytes 1572868
  520.6 4.1 collective-permute-start.2
  521.9 6.8 %collective-permute-start.3 = (bf16[2,1,512,128]{3,2,1,0:T(8,128)(2,1)S(1)}, bf16[2,1,512,128]{3,2,1,0:T(8,128)(2,1)S(1)}, u32[]{:S(2)}, u32[]{:S(2)}) collective-permute-start(bf16[2,1,512,128]{3,2,1,0:T(8,128)(2,1)S(1)} %get-tuple-element.111), channel_id=1, source_target_pairs={{8,0},{16,8},{24,16},{32,24},{40,32},{48,40},{56,48},{64,56},{72,6... | collective-permute-start | bytes 786440 | tf_op jit(solution)/shard_map/ppermute | solution.py:24
  540.8 72.5 %copy-start.6 = (f32[4,512,128]{2,1,0:T(8,128)S(1)}, f32[4,512,128]{2,1,0:T(8,128)}, u32[]{:S(2)}) copy-start(f32[4,512,128]{2,1,0:T(8,128)} %get-tuple-element.122) | copy-start | bytes 3145732
  540.8 72.5 %copy-start.7 = (f32[2048,128]{1,0:T(8,128)S(1)}, f32[2048,128]{1,0:T(8,128)}, u32[]{:S(2)}) copy-start(f32[2048,128]{1,0:T(8,128)} %get-tuple-element.136) | copy-start | bytes 3145732
  540.8 72.5 %copy-start.23 = (f32[1,4,4,128]{3,1,2,0:T(4,128)S(1)}, f32[1,4,4,128]{3,1,2,0:T(4,128)}, u32[]{:S(2)}) copy-start(f32[1,4,4,128]{3,1,2,0:T(4,128)} %copy-done.22) | copy-start | bytes 24580
  540.8 75.3 %copy-start.1 = (bf16[128,1024]{1,0:T(8,128)(2,1)S(1)}, bf16[128,1024]{1,0:T(8,128)(2,1)}, u32[]{:S(2)}) copy-start(bf16[128,1024]{1,0:T(8,128)(2,1)} %param.34) | copy-start | bytes 786436
  (15 other events, 42.5 us)
Sparse Core Ops, SparseCore 0:
  9.6 62.0 all-gather.2
  338.4 55.4 all-gather.4
  540.9 59.7 reduce-scatter.3
where the time goes:
time: 629 us; the launch traced here: 623 us
  waiting for transfers between devices  230 us (37%)
  matrix products  139 us (22%)
  blocking collectives  101 us (16%)
  local copies, waits for them, and re-layouts  73.5 us (12%)
  other arithmetic  36.7 us (6%)
  starting transfers between devices  27.7 us (4%)
  between operations  14.7 us (2%)
    all_gather x1, waiting for transfers between devices, body(): wide_state = lax.all_gather(state, 'chan', axis=2, tiled=True)  63.6 us
    unnamed x4, waiting for transfers between devices  59.7 us
    all_gather x1, waiting for transfers between devices, body(): portion = lax.all_gather(grad_low, 'chan', axis=2, tiled=True)  55.6 us
    all_to_all x1, blocking collectives, sent_and_summed(): lax.all_to_all(in_blocks(array, dim, length), axis, 0, 0, tiled=True)  54.5 us
    all_to_all x2, blocking collectives, from_everyone(): return lax.all_to_all(copies, axis, split_axis=0, concat_axis=0, tiled=True)  47 us
    dot_general x1, matrix products, attend_backward(): jnp.einsum('rwhij,rwihd->rwjhd', grad_scores, queries, preferred_element_...  40.1 us
    dot_general x1, matrix products, attend_backward(): jnp.einsum('rwhij,rwjhd->rwihd', grad_scores, keys_win, preferred_element...  33.2 us
    all_to_all x1, waiting for transfers between devices, from_everyone(): return lax.all_to_all(copies, axis, split_axis=0, concat_axis=0, tiled=True)  29.9 us
  transfers between devices with their start and end apart: 11, of which 8 were waited for; matrix products, arithmetic and copies ran while one was open for 4% of the time, Pallas kernels for 0%

commit v1 on v0

--- a/solution.py
+++ b/solution.py
@@ -172,7 +172,8 @@
     chan_pos = lax.axis_index("chan")
     lat_pos = lax.axis_index("lat")
     lat_count = lax.axis_size("lat")
-    wide_state = lax.all_gather(state, "chan", axis=2, tiled=True)
+    stack = jnp.stack([state] * lax.axis_size("chan"))
+    wide_state = jnp.concatenate(lax.all_to_all(stack, "chan", 0, 0), axis=2)
     hat_rows, inverse = normalize(wide_state.astype(jnp.float32).reshape(tokens, D))
     normed = (hat_rows * gain).astype(jnp.bfloat16)
     queries = jnp.dot(normed, w_query, preferred_element_type=jnp.float32).astype(jnp.bfloat16)

time: 629 us -> 651 us (1.035)
  waiting for transfers between devices: 230 us -> 215 us
  blocking collectives: 101 us -> 113 us
  local copies, waits for them, and re-layouts: 73.5 us -> 82.4 us
    all_gather x1 -> x0, waiting for transfers between devices: 63.6 us -> none  [body(): wide_state = lax.all_gather(state, 'chan', axis=2, tiled=True)]
    all_to_all x0 -> x1, waiting for transfers between devices: none -> 49.4 us  [body(): wide_state = jnp.concatenate(lax.all_to_all(stack, 'chan', 0, 0), axis=2)]
    all_to_all x1, blocking collectives: 54.5 us -> 66.1 us  [sent_and_summed(): lax.all_to_all(in_blocks(array, dim, length), axis, 0, 0, tiled=True)]
    convert_element_type x0 -> x2, other arithmetic: none -> 7.33 us  [the longest x1 4.17 us: body(): normed = (hat_rows * gain).astype(jnp.bfloat16)]
    unnamed x4 -> x3, waiting for transfers between devices: 59.7 us -> 59 us
    unnamed x62 -> x60, local copies, waits for them, and re-layouts: 13.3 us -> 12.8 us
where the time goes in v1:
time: 651 us; the launch traced here: 640 us
  waiting for transfers between devices  215 us (33%)
  matrix products  138 us (21%)
  blocking collectives  113 us (17%)
  local copies, waits for them, and re-layouts  82.4 us (13%)
  other arithmetic  41.7 us (6%)
  starting transfers between devices  34 us (5%)
  between operations  15.3 us (2%)
    all_to_all x1, blocking collectives, sent_and_summed(): lax.all_to_all(in_blocks(array, dim, length), axis, 0, 0, tiled=True)  66.1 us
    unnamed x3, waiting for transfers between devices  59 us
    all_gather x1, waiting for transfers between devices, body(): portion = lax.all_gather(grad_low, 'chan', axis=2, tiled=True)  55.6 us
    all_to_all x1, waiting for transfers between devices, body(): wide_state = jnp.concatenate(lax.all_to_all(stack, 'chan', 0, 0), axis=2)  49.4 us
    all_to_all x2, blocking collectives, from_everyone(): return lax.all_to_all(copies, axis, split_axis=0, concat_axis=0, tiled=True)  46.9 us
    dot_general x1, matrix products, attend_backward(): jnp.einsum('rwhij,rwihd->rwjhd', grad_scores, queries, preferred_element_...  40.2 us
    dot_general x1, matrix products, attend_backward(): jnp.einsum('rwhij,rwjhd->rwihd', grad_scores, keys_win, preferred_element...  32.9 us
    all_to_all x1, waiting for transfers between devices, from_everyone(): return lax.all_to_all(copies, axis, split_axis=0, concat_axis=0, tiled=True)  29.9 us
  transfers between devices with their start and end apart: 11, of which 8 were waited for; matrix products, arithmetic and copies ran while one was open for 4% of the time, Pallas kernels for 0%

profile of v1, /device:TPU:0, one launch (start us, length us, event | category | flops | bytes accessed | tf_op | source)
XLA Modules:
  0.0 639.9 jit_solution(1357922281002577611)
XLA Ops:
  11.2 5.8 all-to-all-start
  17.1 49.4 %all-to-all-done = bf16[8,4,512,128]{3,2,1,0:T(8,128)(2,1)} async-done(((bf16[8,4,512,128]{3,2,1,0:T(8,128)(2,1)}), bf16[8,4,512,128]{3,2,1,0:T(8,128)(2,1)}, u32[]{:S(2)}, u32[]{:S(2)}) %all-to-all-start) | async-done | bytes 4194336 | tf_op jit(solution)/shard_map/all_to_all | solution.py:176
  75.6 4.9 copy.139
  132.6 10.2 %fusion.83 = (f32[4,2,2,256]{3,2,1,0:T(2,128)S(1)}, f32[4,2,2,256,768]{4,3,2,1,0:T(8,128)}) fusion(pred[4,768]{1,0:T(4,128)(4,1)S(1)} %bitcast.254, bf16[4,2,256,2,64]{2,4,3,1,0:T(8,128)(2,1)S(1)} %copy-done.14, bf16[4,2,768,2,64]{2,4,3,1,0:T(8,128)(2,1)} %reshape.534), kind=kOutput, calls=%fused_computation.132 | convolution fusion | flops 415236864 | bytes 14699520 | tf_op jit(solution)/shard_map/sub | solution.py:112
  142.8 6.7 %fusion.42 = bf16[4,2,256,2,64]{2,4,3,1,0:T(8,128)(2,1)S(1)} fusion(bf16[4,2,768,2,64]{2,4,3,1,0:T(8,128)(2,1)S(1)} %copy-done.3, f32[4,2,2,256,768]{4,3,2,1,0:T(8,128)} %get-tuple-element.134, f32[4,2,2,256]{3,2,1,0:T(2,128)S(1)} %get-tuple-element.133), kind=kOutput, calls=%fused_computation.57 | convolution fusion | flops 409206784 | bytes 14696448 | tf_op jit(solution)/shard_map/rwhij,rwjhd->rwihd/dot_general | solution.py:115
  152.8 66.1 %all_to_all.65 = bf16[8,4,512,128]{3,2,1,0:T(8,128)(2,1)} all-to-all(bf16[8,4,512,128]{3,2,1,0:T(8,128)(2,1)S(1)} %bitcast.229), channel_id=1, replica_groups=mesh['lat'=16,'chan'=8] {'chan'}, dimensions={0} | all-to-all | bytes 8388608 | tf_op jit(solution)/shard_map/all_to_all | solution.py:37
  218.9 9.8 %all-to-all-start.3 = ((s32[1,1,16,16]{3,1,0,2:T(1,128)}), s32[1,1,16,16]{3,1,0,2:T(1,128)S(1)}, u32[]{:S(2)}, u32[]{:S(2)}) async-start(s32[1,1,16,16]{3,1,0,2:T(1,128)} %bitcast.15), calls=%async_computation.3 | async-start | bytes 16384 | tf_op jit(solution)/shard_map/all_to_all | solution.py:209
  241.8 29.9 %all-to-all-done.2 = bf16[8,69,2048]{2,1,0:T(8,128)(2,1)S(1)} async-done(((bf16[8,69,2048]{2,1,0:T(8,128)(2,1)}), bf16[8,69,2048]{2,1,0:T(8,128)(2,1)S(1)}, u32[]{:S(2)}, u32[]{:S(2)}) %all-to-all-start.2) | async-done | bytes 2261024 | tf_op jit(solution)/shard_map/all_to_all | solution.py:43
  279.9 6.2 all-to-all-done.4
  286.1 7.8 %fusion.7 = f32[16,16,1,128]{3,2,1,0:T(1,128)S(1)} fusion(bf16[1,1,16,16,128,128]{5,4,3,2,1,0:T(8,128)(2,1)} %param.36, bf16[16,16,128,1]{2,1,0,3:T(8,128)(2,1)S(1)} %bitcast.245), kind=kOutput, calls=%fused_computation.14 | convolution fusion | flops 8388608 | bytes 8585216 | tf_op jit(solution)/shard_map/abcsok,abcsk->abcso/dot_general | solution.py:212
  294.0 5.7 fusion.5
  304.0 7.9 %all-to-all-done.5 = bf16[1,2,16,16,128]{4,3,1,0,2:T(8,128)(2,1)S(1)} async-done(((bf16[1,2,16,16,128]{4,3,1,0,2:T(8,128)(2,1)}), bf16[1,2,16,16,128]{4,3,1,0,2:T(8,128)(2,1)S(1)}, u32[]{:S(2)}, u32[]{:S(2)}) %all-to-all-start.5) | async-done | bytes 131104 | tf_op jit(solution)/shard_map/all_to_all | solution.py:59
  314.4 37.8 %all_to_all.66 = bf16[8,1104,128]{2,1,0:T(8,128)(2,1)S(1)} all-to-all(bf16[8,1104,128]{2,1,0:T(8,128)(2,1)S(1)} %broadcast_in_dim.61), channel_id=1, replica_groups=mesh['lat'=16,'chan'=8] {'chan'}, dimensions={0} | all-to-all | bytes 4521984 | tf_op jit(solution)/shard_map/all_to_all | solution.py:43
  354.9 55.6 %all-gather.2.cloned.1.call-done = bf16[4,512,1024]{2,1,0:T(8,128)(2,1)} async-done(((bf16[4,512,128]{2,1,0:T(8,128)(2,1)}), bf16[4,512,1024]{2,1,0:T(8,128)(2,1)}) %all-gather.2.cloned.1.call-update) | async-done | bytes 4194320 | tf_op jit(solution)/shard_map/all_gather | solution.py:245
  416.3 6.5 %fusion.31 = f32[4,2,768,2,64]{2,4,3,1,0:T(8,128)S(1)} fusion(bf16[4,2,256,2,64]{2,4,3,1,0:T(8,128)(2,1)} %copy.158, f32[4,2,2,256,768]{4,3,2,1,0:T(8,128)} %get-tuple-element.134, f32[4,2,2,256]{3,2,1,0:T(2,128)S(1)} %get-tuple-element.133), kind=kOutput, calls=%fused_computation.49 | convolution fusion | flops 408944640 | bytes 16269312 | tf_op jit(solution)/shard_map/rwhij,rwihd->rwjhd/dot_general | solution.py:133
  422.9 6.3 fusion.85
  429.2 32.9 %fusion.45 = bf16[4,2,256,2,64]{2,4,3,1,0:T(8,128)(2,1)} fusion(bf16[4,2,768,2,64]{2,4,3,1,0:T(8,128)(2,1)} %reshape.534, f32[4,2,2,256,768]{4,3,2,1,0:T(8,128)} %fusion.85, f32[4,2,2,256,768]{4,3,2,1,0:T(8,128)} %get-tuple-element.134, f32[4,2,2,256]{3,2,1,0:T(2,128)S(1)} %get-tuple-element.133), kind=kOutput, calls=%fused_computation.58 | convolution fusion | flops 424940288 | bytes 27279360 | tf_op jit(solution)/shard_map/rwhij,rwjhd->rwihd/dot_general | solution.py:127
  462.1 40.2 %fusion.28 = f32[4,2,768,2,64]{2,4,3,1,0:T(8,128)} fusion(bf16[4,2,256,2,64]{2,4,3,1,0:T(8,128)(2,1)} %copy.149, f32[4,2,2,256,768]{4,3,2,1,0:T(8,128)} %fusion.85, f32[4,2,2,256,768]{4,3,2,1,0:T(8,128)} %get-tuple-element.134, f32[4,2,2,256]{3,2,1,0:T(2,128)S(1)} %get-tuple-element.133), kind=kOutput, calls=%fused_computation.48 | convolution fusion | flops 424678144 | bytes 28852224 | tf_op jit(solution)/shard_map/rwhij,rwihd->rwjhd/dot_general | solution.py:130
  502.3 5.9 reshape.549
  508.3 4.9 copy.181
  513.2 4.9 copy.161
  550.7 6.6 %copy.186 = bf16[2048,1024]{0,1:T(8,128)(2,1)} copy(bf16[2048,1024]{1,0:T(8,128)(2,1)} %add_convert_fusion) | data formatting | bytes 8388608
  558.2 59.0 %reduce-scatter.4.cloned.1.call-done = bf16[128,2048]{1,0:T(8,128)(2,1)} async-done(((bf16[1024,2048]{1,0:T(8,128)(2,1)}), bf16[128,2048]{1,0:T(8,128)(2,1)}) %reduce-scatter.4.cloned.1.call-update) | async-done | bytes 524304
  620.4 9.1 %all_to_all.67 = f32[8,1,4096]{2,1,0:T(1,128)S(1)} all-to-all(f32[8,1,4096]{2,1,0:T(1,128)S(1)} %broadcast_in_dim.62), channel_id=1, replica_groups=mesh['lat'=16,'chan'=8] {'chan'}, dimensions={0} | all-to-all | bytes 262144 | tf_op jit(solution)/shard_map/all_to_all | solution.py:43
  (169 shorter events, 144.6 us)
Async XLA Ops:
  7.2 143.2 %copy-start = (bf16[128,1024]{1,0:T(8,128)(2,1)S(1)}, bf16[128,1024]{1,0:T(8,128)(2,1)}, u32[]{:S(2)}) copy-start(bf16[128,1024]{1,0:T(8,128)(2,1)} %param.34) | copy-start | bytes 786436
  11.2 55.3 %all-to-all-start = ((bf16[8,4,512,128]{3,2,1,0:T(8,128)(2,1)}), bf16[8,4,512,128]{3,2,1,0:T(8,128)(2,1)}, u32[]{:S(2)}, u32[]{:S(2)}) async-start(bf16[8,4,512,128]{3,2,1,0:T(8,128)(2,1)} %stack.71), calls=%async_computation | async-start | bytes 8388608 | tf_op jit(solution)/shard_map/all_to_all | solution.py:176
  72.4 8.1 %copy-start.21 = (f32[1,4,4,128]{3,1,2,0:T(4,128)}, f32[1,4,4,128]{3,1,2,0:T(4,128)S(1)}, u32[]{:S(2)}) copy-start(f32[1,4,4,128]{3,1,2,0:T(4,128)S(1)} %copy.199) | copy-start | bytes 24580
  95.0 18.5 %collective-permute-start = (bf16[2,1,512,128]{2,3,1,0:T(8,128)(2,1)}, bf16[2,1,512,128]{2,3,1,0:T(8,128)(2,1)}, u32[]{:S(2)}, u32[]{:S(2)}) collective-permute-start(bf16[2,1,512,128]{2,3,1,0:T(8,128)(2,1)} %get-tuple-element.120), channel_id=1, source_target_pairs={{0,8},{8,16},{16,24},{24,32},{32,40},{40,48},{48,56},{56,64},{64,7... | collective-permute-start | bytes 786440 | tf_op jit(solution)/shard_map/ppermute | solution.py:23
  97.3 16.1 %collective-permute-start.1 = (bf16[2,1,512,128]{2,3,1,0:T(8,128)(2,1)}, bf16[2,1,512,128]{2,3,1,0:T(8,128)(2,1)}, u32[]{:S(2)}, u32[]{:S(2)}) collective-permute-start(bf16[2,1,512,128]{2,3,1,0:T(8,128)(2,1)} %get-tuple-element.121), channel_id=1, source_target_pairs={{8,0},{16,8},{24,16},{32,24},{40,32},{48,40},{56,48},{64,56},{72,6... | collective-permute-start | bytes 786440 | tf_op jit(solution)/shard_map/ppermute | solution.py:24
  132.6 10.2 %copy-start.3 = (bf16[4,2,768,2,64]{2,4,3,1,0:T(8,128)(2,1)S(1)}, bf16[4,2,768,2,64]{2,4,3,1,0:T(8,128)(2,1)}, u32[]{:S(2)}) copy-start(bf16[4,2,768,2,64]{2,4,3,1,0:T(8,128)(2,1)} %reshape.532) | copy-start | bytes 4718596
  218.9 12.7 %copy-start.9 = (bf16[4,512,128]{2,1,0:T(8,128)(2,1)S(1)}, bf16[4,512,128]{2,1,0:T(8,128)(2,1)}, u32[]{:S(2)}) copy-start(bf16[4,512,128]{2,1,0:T(8,128)(2,1)} %param.28) | copy-start | bytes 1572868
  218.9 12.7 %copy-start.13 = (bf16[4,512,128]{2,1,0:T(8,128)(2,1)S(1)}, bf16[4,512,128]{2,1,0:T(8,128)(2,1)}, u32[]{:S(2)}) copy-start(bf16[4,512,128]{2,1,0:T(8,128)(2,1)} %param.29) | copy-start | bytes 1572868
  218.9 17.3 %all-to-all-start.3 = ((s32[1,1,16,16]{3,1,0,2:T(1,128)}), s32[1,1,16,16]{3,1,0,2:T(1,128)S(1)}, u32[]{:S(2)}, u32[]{:S(2)}) async-start(s32[1,1,16,16]{3,1,0,2:T(1,128)} %bitcast.15), calls=%async_computation.3 | async-start | bytes 16384 | tf_op jit(solution)/shard_map/all_to_all | solution.py:209
  237.9 40.5 %copy-start.26 = (s32[1,1,16]{2,1,0:T(1,128)S(1)}, s32[1,1,16]{2,1,0:T(1,128)}, u32[]{:S(2)}) copy-start(s32[1,1,16]{2,1,0:T(1,128)} %param.39) | copy-start | bytes 196
  237.9 33.7 %all-to-all-start.2 = ((bf16[8,69,2048]{2,1,0:T(8,128)(2,1)}), bf16[8,69,2048]{2,1,0:T(8,128)(2,1)S(1)}, u32[]{:S(2)}, u32[]{:S(2)}) async-start(bf16[8,69,2048]{2,1,0:T(8,128)(2,1)} %broadcast_in_dim.58), calls=%async_computation.2 | async-start | bytes 4718592 | tf_op jit(solution)/shard_map/all_to_all | solution.py:43
  273.7 12.3 %all-to-all-start.4 = ((bf16[16,1,1,16,128]{4,3,2,1,0:T(8,128)(2,1)}), bf16[16,1,1,16,128]{4,3,2,1,0:T(8,128)(2,1)S(1)}, u32[]{:S(2)}, u32[]{:S(2)}) async-start(bf16[16,1,1,16,128]{4,3,2,1,0:T(8,128)(2,1)} %bitcast.18), calls=%async_computation.4 | async-start | bytes 131072 | tf_op jit(solution)/shard_map/all_to_all | solution.py:211
  286.1 7.8 %copy-start.24 = (bf16[1,1,16,16,128]{4,3,2,1,0:T(8,128)(2,1)S(1)}, bf16[1,1,16,16,128]{4,3,2,1,0:T(8,128)(2,1)}, u32[]{:S(2)}) copy-start(bf16[1,1,16,16,128]{4,3,2,1,0:T(8,128)(2,1)} %param.37) | copy-start | bytes 196612
  300.4 11.5 %all-to-all-start.5 = ((bf16[1,2,16,16,128]{4,3,1,0,2:T(8,128)(2,1)}), bf16[1,2,16,16,128]{4,3,1,0,2:T(8,128)(2,1)S(1)}, u32[]{:S(2)}, u32[]{:S(2)}) async-start(bf16[1,2,16,16,128]{4,3,1,0,2:T(8,128)(2,1)} %pad_maximum_fusion.12), calls=%async_computation.5 | async-start | bytes 262144 | tf_op jit(solution)/shard_map/all_to_all | solution.py:59
  303.9 106.6 %all-gather.2.cloned.1.call-start = ((), (), s32[]{:S(2)}) async-start(), calls=%async_computation.9 | async-start | bytes 4718592 | tf_op jit(solution)/shard_map/all_gather | solution.py:245
  354.9 262.3 %reduce-scatter.4.cloned.1.call-start = ((), (), s32[]{:S(2)}) async-start(), calls=%async_computation.10 | async-start | bytes 4718592
  416.3 6.5 %copy-start.4 = (bf16[4,2,768,2,64]{2,4,3,1,0:T(8,128)(2,1)S(1)}, bf16[4,2,768,2,64]{2,4,3,1,0:T(8,128)(2,1)}, u32[]{:S(2)}) copy-start(bf16[4,2,768,2,64]{2,4,3,1,0:T(8,128)(2,1)} %reshape.532) | copy-start | bytes 4718596
  416.3 6.6 %copy-start.10 = (bf16[4,2,256,2,64]{2,4,3,1,0:T(8,128)(2,1)S(1)}, bf16[4,2,256,2,64]{2,4,3,1,0:T(8,128)(2,1)}, u32[]{:S(2)}) copy-start(bf16[4,2,256,2,64]{2,4,3,1,0:T(8,128)(2,1)} %copy.158) | copy-start | bytes 1572868
  537.1 4.1 collective-permute-start.2
  538.4 6.8 %collective-permute-start.3 = (bf16[2,1,512,128]{3,2,1,0:T(8,128)(2,1)S(1)}, bf16[2,1,512,128]{3,2,1,0:T(8,128)(2,1)S(1)}, u32[]{:S(2)}, u32[]{:S(2)}) collective-permute-start(bf16[2,1,512,128]{3,2,1,0:T(8,128)(2,1)S(1)} %get-tuple-element.111), channel_id=1, source_target_pairs={{8,0},{16,8},{24,16},{32,24},{40,32},{48,40},{56,48},{64,56},{72,6... | collective-permute-start | bytes 786440 | tf_op jit(solution)/shard_map/ppermute | solution.py:24
  557.2 72.4 %copy-start.6 = (f32[4,512,128]{2,1,0:T(8,128)S(1)}, f32[4,512,128]{2,1,0:T(8,128)}, u32[]{:S(2)}) copy-start(f32[4,512,128]{2,1,0:T(8,128)} %get-tuple-element.122) | copy-start | bytes 3145732
  557.2 72.5 %copy-start.7 = (f32[2048,128]{1,0:T(8,128)S(1)}, f32[2048,128]{1,0:T(8,128)}, u32[]{:S(2)}) copy-start(f32[2048,128]{1,0:T(8,128)} %get-tuple-element.136) | copy-start | bytes 3145732
  557.3 72.5 %copy-start.22 = (f32[1,4,4,128]{3,1,2,0:T(4,128)S(1)}, f32[1,4,4,128]{3,1,2,0:T(4,128)}, u32[]{:S(2)}) copy-start(f32[1,4,4,128]{3,1,2,0:T(4,128)} %copy-done.21) | copy-start | bytes 24580
  557.3 75.3 %copy-start.1 = (bf16[128,1024]{1,0:T(8,128)(2,1)S(1)}, bf16[128,1024]{1,0:T(8,128)(2,1)}, u32[]{:S(2)}) copy-start(bf16[128,1024]{1,0:T(8,128)(2,1)} %param.34) | copy-start | bytes 786436
  (14 other events, 40.4 us)
Sparse Core Ops, SparseCore 0:
  355.0 55.4 all-gather.1
  557.4 59.7 reduce-scatter.3
